TPU v7x, 32 devices: a whole 2x2x4 slice. The times are simulated.
32 devices in a mesh: segment: 2 (over x), blk: 4 (over z), mp: 4 (over y, core).
Axes of the slice: x: 2, y: 2, z: 4, core: 2. Of those that a mesh axis runs over, the one named last changes fastest.
Arguments:
- segment_in: bfloat16 [2, 1024, 4096], P('segment', 'blk'), may hold values from -7.5 to 7.5
- norm_gains: float32 [2, 4096], P('segment'), may hold values from 0.25 to 1.75
- projections: bfloat16 [2, 4096, 2, 2048], P('segment', None, None, 'mp'), may hold values from -2 to 2
- live_counts: int32 [2, 4], P(None, 'blk'), may hold values from 1 to 256, 768 in all within a row
- cotangent: bfloat16 [1024, 4096], P('blk', 'mp'), may hold values from -6 to 6
Outputs:
- segment_out: bfloat16 [2, 1024, 4096], P('segment', 'blk', 'mp')
- state_grads: bfloat16 [2, 1024, 4096], P('segment', 'blk', 'mp')
Inputs may be any that keep to these rules, and one draw needn't show every extreme that they name: `live_counts`: each row sums to 768; every entry is at least 1; each row has an entry equal to 256.
All inputs are finite; a program needn't handle non-finite values. No bound on the sum of `live_counts` on one device may be relied on, other than what follows from the above.
Results may differ from a plain program's by a relative error of at most 0.015.
Values may be sent and summed in bfloat16 or wider, within the bound.
No kernel may reach another device: no remote copies, remote signals or barrier semaphores. Data moves between devices by JAX's collectives and lax.ppermute only.
A program may use at most 128 MiB of HBM per device.

v0:
```python
import jax
import jax.numpy as jnp
from jax import lax
from jax.sharding import PartitionSpec as P

DH = 64
WIN = 4
EPSILON = 1e-06
SCALE = 0.125
NEGATIVE = -1e30


def from_behind(x, axis, by):
    size = lax.axis_size(axis)
    pairs = [(i, i + by) for i in range(size) if 0 <= i + by < size]
    return lax.ppermute(x, axis, pairs)


def normalize(states, gain_row):
    widened = states.astype(jnp.float32)
    spread = jnp.sqrt(jnp.mean(widened * widened, axis=-1, keepdims=True) + EPSILON)
    return ((widened / spread * gain_row).astype(jnp.bfloat16), spread)


def right_product(left, right):
    return lax.dot_general(
        left, right, (((1,), (1,)), ((), ())), preferred_element_type=jnp.float32
    )


def per_device(segment_in, norm_gains, projections, live_counts, cotangent):
    segment_pos = lax.axis_index("segment")
    model_index = lax.axis_index("mp")
    states = segment_in[0]
    gain_row = norm_gains[0]
    row_count, full_width = states.shape
    feature_width = cotangent.shape[1]
    w_primary = projections[0, :, 0, :]
    w_secondary = projections[0, :, 1, :]
    group_width = w_primary.shape[1]
    group_heads = group_width // DH
    normed, spread = normalize(states, gain_row)
    primary = jnp.dot(normed, w_primary, preferred_element_type=jnp.float32).astype(jnp.bfloat16)
    secondary = lax.cond(
        segment_pos == 0,
        lambda: jnp.dot(normed, w_secondary, preferred_element_type=jnp.float32).astype(
            jnp.bfloat16
        ),
        lambda: jnp.zeros_like(primary),
    )
    doc_keys, doc_values = from_behind((primary, secondary), "segment", 1)
    own_block = (doc_keys, doc_values, live_counts[0])
    window = [own_block]
    moving = own_block
    for offset in range(1, WIN):
        moving = from_behind((moving[0], moving[1], moving[2]), "blk", 1)
        window.append(moving)
    position = jnp.arange(row_count, dtype=jnp.int32)
    all_keys = jnp.concatenate([piece[0] for piece in window], 0).reshape(
        WIN * row_count, group_heads, DH
    )
    all_values = jnp.concatenate([piece[1] for piece in window], 0).reshape(
        WIN * row_count, group_heads, DH
    )
    key_live = jnp.concatenate([position < piece[2][0] for piece in window], 0)
    query_live = position < live_counts[1][0]
    query_heads = primary.reshape(row_count, group_heads, DH)
    scores = (
        jnp.einsum("qhd,khd->hqk", query_heads, all_keys, preferred_element_type=jnp.float32)
        * SCALE
    )
    scores = jnp.where(key_live[None, None, :], scores, NEGATIVE)
    row_max = jnp.max(scores, axis=-1, keepdims=True)
    expo = jnp.exp(scores - row_max)
    row_total = jnp.sum(expo, axis=-1, keepdims=True)
    softmax_out = expo / row_total
    weights_low = softmax_out.astype(jnp.bfloat16)
    attended = jnp.einsum(
        "hqk,khd->qhd", weights_low, all_values, preferred_element_type=jnp.float32
    ).astype(jnp.bfloat16)
    attended = jnp.where(query_live[:, None, None], attended, jnp.zeros_like(attended)).reshape(
        row_count, group_width
    )
    projected = lax.cond(
        segment_pos == 1,
        lambda: right_product(attended, w_secondary),
        lambda: jnp.zeros((row_count, full_width), jnp.float32),
    )
    layer_out = lax.psum_scatter(
        projected.astype(jnp.bfloat16), "mp", scatter_dimension=1, tiled=True
    )
    own_normed = lax.dynamic_slice_in_dim(normed, model_index * feature_width, feature_width, 1)
    segment_out = jnp.where(segment_pos == 0, own_normed, layer_out)[None]
    grad_out = jnp.dot(
        lax.all_gather(cotangent, "mp", axis=1, tiled=True),
        w_secondary,
        preferred_element_type=jnp.float32,
    )
    grad_out = grad_out.astype(jnp.bfloat16)
    grad_out = jnp.where(query_live[:, None], grad_out, jnp.zeros_like(grad_out))
    grad_heads = grad_out.reshape(row_count, group_heads, DH)
    grad_probs = jnp.einsum(
        "qhd,khd->hqk", grad_heads, all_values, preferred_element_type=jnp.float32
    )
    row_delta = jnp.sum(softmax_out * grad_probs, axis=-1, keepdims=True)
    grad_scores = (softmax_out * (grad_probs - row_delta)).astype(jnp.bfloat16)
    grad_queries = (
        (
            SCALE
            * jnp.einsum("hqk,khd->qhd", grad_scores, all_keys, preferred_element_type=jnp.float32)
        )
        .astype(jnp.bfloat16)
        .reshape(row_count, group_width)
    )
    key_parts = (
        SCALE
        * jnp.einsum("hqk,qhd->khd", grad_scores, query_heads, preferred_element_type=jnp.float32)
    ).reshape(WIN, row_count, group_width)
    value_parts = jnp.einsum(
        "hqk,qhd->khd", weights_low, grad_heads, preferred_element_type=jnp.float32
    ).reshape(WIN, row_count, group_width)
    key_total = key_parts[WIN - 1]
    value_total = value_parts[WIN - 1]
    for offset in range(WIN - 2, -1, -1):
        arrived = (
            from_behind(key_total.astype(jnp.bfloat16), "blk", -1).astype(key_total.dtype),
            from_behind(value_total.astype(jnp.bfloat16), "blk", -1).astype(value_total.dtype),
        )
        key_total = arrived[0] + key_parts[offset]
        value_total = arrived[1] + value_parts[offset]
    grad_keys = key_total.astype(jnp.bfloat16)
    grad_values = value_total.astype(jnp.bfloat16)
    back_keys, back_values = from_behind((grad_keys, grad_values), "segment", -1)
    partial_grad = lax.cond(
        segment_pos == 0,
        lambda: right_product(back_keys, w_primary) + right_product(back_values, w_secondary),
        lambda: right_product(grad_queries, w_primary),
    )
    widened = states.astype(jnp.float32)
    summed = lax.psum_scatter(
        partial_grad.astype(jnp.bfloat16), "mp", scatter_dimension=1, tiled=True
    ).astype(jnp.float32)
    own_states = lax.dynamic_slice_in_dim(widened, model_index * feature_width, feature_width, 1)
    own_gain = lax.dynamic_slice_in_dim(gain_row, model_index * feature_width, feature_width, 0)
    row_term = lax.psum(jnp.sum(summed * own_gain * own_states, axis=-1, keepdims=True), "mp")
    input_grad = (
        own_gain * summed / spread - own_states * row_term / (full_width * spread**3)
    ).astype(jnp.bfloat16)
    return (segment_out, input_grad[None])


def solution(mesh):
    in_specs = (
        P("segment", "blk", None),
        P("segment", None),
        P("segment", None, None, "mp"),
        P(None, "blk"),
        P("blk", "mp"),
    )
    out_specs = (P("segment", "blk", "mp"), P("segment", "blk", "mp"))
    return jax.shard_map(
        per_device, mesh=mesh, in_specs=in_specs, out_specs=out_specs, check_vma=False
    )
```

profile of v0, /device:TPU:0, one launch (start us, length us, event | category | flops | bytes accessed | tf_op | source)
XLA Modules:
  0.0 235.8 jit_solution(16366591640232580074)
XLA Ops:
  9.3 17.6 %fusion.40 = (bf16[1,4096,1,512]{3,2,1,0:T(2,128)(2,1)}, bf16[1,4096,1,512]{3,2,1,0:T(2,128)(2,1)S(1)}) fusion(bf16[1,4096,2,512]{3,2,1,0:T(2,128)(2,1)} %param.13), kind=kLoop, calls=%fused_computation.70 | loop fusion | bytes 16777216 | tf_op jit(solution)/shard_map/slice | solution.py:38
  27.0 3.3 %copy.45 = bf16[1,4096,1,512]{3,1,2,0:T(8,128)(2,1)} copy(bf16[1,4096,1,512]{3,2,1,0:T(2,128)(2,1)S(1)} %get-tuple-element.63) | data formatting | bytes 8388608
  32.3 4.1 %conditional.3 = (bf16[256,512]{1,0:T(8,128)(2,1)S(1)}) conditional(s32[]{:T(128)} %convert_element_type.110, () %tuple.27, (bf16[256,4096]{1,0:T(8,128)(2,1)}, bf16[4096,512]{1,0:T(8,128)(2,1)}) %tuple.58), branch_computations={%region_1.0_spmd, %region_2.0_spmd} | conditional | flops 1073872896 | bytes 6553608 | solution.py:44
  32.3 4.1 %convolution_convert_fusion = bf16[256,512]{1,0:T(8,128)(2,1)S(1)} fusion(bf16[256,4096]{1,0:T(8,128)(2,1)} %get-tuple-element.42, bf16[4096,512]{1,0:T(8,128)(2,1)} %get-tuple-element.43), kind=kOutput, calls=%fused_computation | convolution fusion | flops 1073872896 | bytes 6553600 | tf_op jit(solution)/shard_map/cond/branch_1_fun/dot_general | solution.py:46
  37.7 4.6 %copy.44 = bf16[1,4096,1,512]{3,1,2,0:T(8,128)(2,1)S(1)} copy(bf16[1,4096,1,512]{3,2,1,0:T(2,128)(2,1)} %get-tuple-element.62) | data formatting | bytes 8388608
  45.6 5.0 %collective-permute-start.1 = (bf16[256,512]{1,0:T(8,128)(2,1)S(1)}, bf16[256,512]{1,0:T(8,128)(2,1)S(1)}, u32[]{:S(2)}, u32[]{:S(2)}) collective-permute-start(bf16[256,512]{1,0:T(8,128)(2,1)S(1)} %collective-permute-done), channel_id=1, source_target_pairs={{0,4},{4,8},{8,12},{1,5},{5,9},{9,13},{2,6},{6,10},{10,14},{3,7},{... | collective-permute-start | bytes 786440 | tf_op jit(solution)/shard_map/ppermute | solution.py:16
  52.0 4.3 %collective-permute-start.8 = (bf16[256,512]{1,0:T(8,128)(2,1)S(1)}, bf16[256,512]{1,0:T(8,128)(2,1)S(1)}, u32[]{:S(2)}, u32[]{:S(2)}) collective-permute-start(bf16[256,512]{1,0:T(8,128)(2,1)S(1)} %collective-permute-done.7), channel_id=1, source_target_pairs={{0,4},{4,8},{8,12},{1,5},{5,9},{9,13},{2,6},{6,10},{10,14},{3,7},{... | collective-permute-start | bytes 786440 | tf_op jit(solution)/shard_map/ppermute | solution.py:16
  57.0 4.0 %collective-permute-start.4 = (s32[1]{0:T(128)}, s32[1]{0:T(128)}, u32[]{:S(2)}, u32[]{:S(2)}) collective-permute-start(s32[1]{0:T(128)} %bitcast.8), channel_id=1, source_target_pairs={{0,4},{4,8},{8,12},{1,5},{5,9},{9,13},{2,6},{6,10},{10,14},{3,7},{... | collective-permute-start | bytes 20 | tf_op jit(solution)/shard_map/ppermute | solution.py:16
  61.0 3.7 %collective-permute-start.2 = (bf16[256,512]{1,0:T(8,128)(2,1)S(1)}, bf16[256,512]{1,0:T(8,128)(2,1)}, u32[]{:S(2)}, u32[]{:S(2)}) collective-permute-start(bf16[256,512]{1,0:T(8,128)(2,1)S(1)} %collective-permute-done.1), channel_id=1, source_target_pairs={{0,4},{4,8},{8,12},{1,5},{5,9},{9,13},{2,6},{6,10},{10,14},{3,7},{... | collective-permute-start | bytes 786440 | tf_op jit(solution)/shard_map/ppermute | solution.py:16
  68.1 3.2 %collective-permute-start.5 = (s32[1]{0:T(128)}, s32[1]{0:T(128)}, u32[]{:S(2)}, u32[]{:S(2)}) collective-permute-start(s32[1]{0:T(128)} %collective-permute-done.4), channel_id=1, source_target_pairs={{0,4},{4,8},{8,12},{1,5},{5,9},{9,13},{2,6},{6,10},{10,14},{3,7},{... | collective-permute-start | bytes 20 | tf_op jit(solution)/shard_map/ppermute | solution.py:16
  71.9 3.8 %collective-permute-start.3 = (bf16[256,512]{1,0:T(8,128)(2,1)}, bf16[256,512]{1,0:T(8,128)(2,1)S(1)}, u32[]{:S(2)}, u32[]{:S(2)}) collective-permute-start(bf16[256,512]{1,0:T(8,128)(2,1)} %collective-permute-done.2), channel_id=1, source_target_pairs={{0,4},{4,8},{8,12},{1,5},{5,9},{9,13},{2,6},{6,10},{10,14},{3,7},{... | collective-permute-start | bytes 786440 | tf_op jit(solution)/shard_map/ppermute | solution.py:16
  76.5 4.2 %collective-permute-start.6 = (s32[1]{0:T(128)}, s32[1]{0:T(128)}, u32[]{:S(2)}, u32[]{:S(2)}) collective-permute-start(s32[1]{0:T(128)} %collective-permute-done.5), channel_id=1, source_target_pairs={{0,4},{4,8},{8,12},{1,5},{5,9},{9,13},{2,6},{6,10},{10,14},{3,7},{... | collective-permute-start | bytes 20 | tf_op jit(solution)/shard_map/ppermute | solution.py:16
  80.7 2.9 %collective-permute-start.10 = (bf16[256,512]{1,0:T(8,128)(2,1)}, bf16[256,512]{1,0:T(8,128)(2,1)}, u32[]{:S(2)}, u32[]{:S(2)}) collective-permute-start(bf16[256,512]{1,0:T(8,128)(2,1)} %collective-permute-done.9), channel_id=1, source_target_pairs={{0,4},{4,8},{8,12},{1,5},{5,9},{9,13},{2,6},{6,10},{10,14},{3,7},{... | collective-permute-start | bytes 786440 | tf_op jit(solution)/shard_map/ppermute | solution.py:16
  89.7 7.4 %fusion.44 = (f32[8,256]{1,0:T(8,128)S(1)}, f32[8,256,1024]{2,1,0:T(8,128)}) fusion(pred[1024]{0:T(1024)(128)(4,1)S(1)} %pad_add_fusion, bf16[256,8,64]{0,2,1:T(8,128)(2,1)S(1)} %bitcast.110, bf16[1024,8,64]{0,2,1:T(8,128)(2,1)} %bitcast.101), kind=kOutput, calls=%fused_computation.74 | convolution fusion | flops 276825088 | bytes 9708544 | tf_op jit(solution)/shard_map/sub | solution.py:74
  97.0 5.6 %fusion.25 = bf16[256,8,64]{0,2,1:T(8,128)(2,1)} fusion(bf16[1024,8,64]{0,2,1:T(8,128)(2,1)S(1)} %bitcast.112, f32[8,256,1024]{2,1,0:T(8,128)} %get-tuple-element.75, f32[8,256]{1,0:T(8,128)S(1)} %get-tuple-element.74), kind=kOutput, calls=%fused_computation.35 | convolution fusion | flops 272760832 | bytes 9707520 | tf_op jit(solution)/shard_map/hqk,khd->qhd/dot_general | solution.py:78
  104.3 4.8 %fusion.29 = bf16[256,512]{1,0:T(8,128)(2,1)} fusion(bf16[256,4096]{1,0:T(8,128)(2,1)} %all-gather.2.cloned.1.call-done, bf16[4096,512]{1,0:T(8,128)(2,1)} %bitcast.97, pred[256]{0:T(512)(128)(4,1)S(1)} %iota_compare_fusion), kind=kOutput, calls=%fused_computation.37 | convolution fusion | flops 1074003968 | bytes 6553856 | tf_op jit(solution)/shard_map/dot_general | solution.py:94
  110.9 5.1 %multiply_reduce_fusion = (f32[8,256]{1,0:T(8,128)S(1)}, f32[8,256,1024]{2,1,0:T(8,128)S(1)}) fusion(f32[8,256,1024]{2,1,0:T(8,128)} %get-tuple-element.75, f32[8,256]{1,0:T(8,128)S(1)} %get-tuple-element.74, bf16[256,8,64]{0,2,1:T(8,128)(2,1)} %bitcast.117, bf16[1024,8,64]{0,2,1:T(8,128)(2,1)S(1)} %bitcast.113), kind=kOutput, calls=%fused_computation.6 | convolution fusion | flops 274724864 | bytes 18104320 | tf_op jit(solution)/shard_map/qhd,khd->hqk/dot_general | solution.py:102
  124.3 4.5 %fusion.15 = f32[1024,8,64]{0,2,1:T(8,128)S(1)} fusion(bf16[256,8,64]{0,2,1:T(8,128)(2,1)S(1)} %bitcast.118, f32[8,256,1024]{2,1,0:T(8,128)} %get-tuple-element.75, f32[8,256]{1,0:T(8,128)S(1)} %get-tuple-element.74), kind=kOutput, calls=%fused_computation.29 | convolution fusion | flops 272629760 | bytes 10756096 | tf_op jit(solution)/shard_map/hqk,qhd->khd/dot_general | solution.py:119
  167.0 3.6 %fusion.28 = bf16[256,8,64]{0,2,1:T(8,128)(2,1)S(1)} fusion(bf16[1024,8,64]{0,2,1:T(8,128)(2,1)S(1)} %bitcast.102, bf16[8,256,1024]{2,1,0:T(8,128)(2,1)} %copy-done.3), kind=kOutput, calls=%fused_computation.36 | convolution fusion | flops 268697600 | bytes 5505024 | tf_op jit(solution)/shard_map/hqk,khd->qhd/dot_general | solution.py:110
  170.6 7.4 %collective-permute-done.14 = bf16[256,512]{1,0:T(8,128)(2,1)S(1)} collective-permute-done((bf16[256,512]{1,0:T(8,128)(2,1)S(1)}, bf16[256,512]{1,0:T(8,128)(2,1)S(1)}, u32[]{:S(2)}, u32[]{:S(2)}) %collective-permute-start.14) | collective-permute-done | bytes 262176 | tf_op jit(solution)/shard_map/ppermute | solution.py:16
  180.8 6.1 %conditional.5 = (bf16[256,4096]{1,0:T(8,128)(2,1)}) conditional(s32[]{:T(128)} %convert_element_type.110, (bf16[256,8,64]{0,2,1:T(8,128)(2,1)S(1)}, bf16[4096,512]{1,0:T(8,128)(2,1)S(1)}) %tuple.56, (bf16[256,512]{1,0:T(8,128)(2,1)S(1)}, bf16[4096,512]{1,0:T(8,128)(2,1)S(1)}, bf16[256,512]{1,0:T(8,128)(2,1)S(1)}, ...), branch_computations={%region_9.10_spmd, %region_10.11_spmd} | conditional | flops 2149580800 | bytes 39321720 | solution.py:134
  184.1 2.8 %convolution_add_fusion = bf16[256,4096]{1,0:T(8,128)(2,1)} fusion(f32[256,4096]{1,0:T(8,128)S(1)} %fusion.46, bf16[256,512]{1,0:T(8,128)(2,1)S(1)} %copy-done.17, bf16[4096,512]{1,0:T(8,128)(2,1)S(1)} %copy-done.2), kind=kOutput, calls=%fused_computation.1 | convolution fusion | flops 1075838976 | bytes 10747904 | tf_op jit(solution)/shard_map/cond/branch_1_fun/dot_general | solution.py:26
  191.5 28.0 %reduce-scatter.5.cloned.1.call-done = bf16[256,1024]{1,0:T(8,128)(2,1)} async-done(((bf16[256,4096]{1,0:T(8,128)(2,1)}), bf16[256,1024]{1,0:T(8,128)(2,1)}) %reduce-scatter.5.cloned.1.call-update) | async-done | bytes 524304 | tf_op jit(solution)/shard_map/reduce_scatter | solution.py:140
  221.1 5.8 %psum.7 = f32[256]{0:T(256)S(1)} all-reduce(f32[256]{0:T(256)S(1)} %fusion.30), channel_id=1, replica_groups=mesh['segment'=2,'blk'=4,'mp'=4] {'mp'}, use_global_device_ids=true, to_apply=%region_13.14 | all-reduce | flops 256 | bytes 2048 | tf_op jit(solution)/shard_map/psum | solution.py:145
  (128 shorter events, 87.6 us)
Async XLA Ops:
  7.2 97.1 %all-gather.2.cloned.1.call-start = ((), (), s32[]{:S(2)}) async-start(), calls=%async_computation.3 | async-start | bytes 2621440 | tf_op jit(solution)/shard_map/all_gather | solution.py:95
  36.3 9.2 %collective-permute-start = (bf16[256,512]{1,0:T(8,128)(2,1)S(1)}, bf16[256,512]{1,0:T(8,128)(2,1)S(1)}, u32[]{:S(2)}, u32[]{:S(2)}) collective-permute-start(bf16[256,512]{1,0:T(8,128)(2,1)S(1)} %get-tuple-element.78), channel_id=1, source_target_pairs={{0,16},{1,17},{2,18},{3,19},{4,20},{5,21},{6,22},{7,23},{8,24},{9,... | collective-permute-start | bytes 786440 | tf_op jit(solution)/shard_map/ppermute | solution.py:16
  37.7 151.8 %reduce-scatter.3.cloned.1.call-start = ((), (), s32[]{:S(2)}) async-start(), calls=%async_computation.2 | async-start | bytes 2621440 | tf_op jit(solution)/shard_map/reduce_scatter | solution.py:89
  44.3 7.8 %collective-permute-start.7 = (bf16[256,512]{1,0:T(8,128)(2,1)S(1)}, bf16[256,512]{1,0:T(8,128)(2,1)S(1)}, u32[]{:S(2)}, u32[]{:S(2)}) collective-permute-start(bf16[256,512]{1,0:T(8,128)(2,1)S(1)} %fusion.22), channel_id=1, source_target_pairs={{0,16},{1,17},{2,18},{3,19},{4,20},{5,21},{6,22},{7,23},{8,24},{9,... | collective-permute-start | bytes 786440 | tf_op jit(solution)/shard_map/ppermute | solution.py:16
  45.6 38.7 %copy-start.12 = (bf16[256,512]{1,0:T(8,128)(2,1)}, bf16[256,512]{1,0:T(8,128)(2,1)S(1)}, u32[]{:S(2)}) copy-start(bf16[256,512]{1,0:T(8,128)(2,1)S(1)} %collective-permute-done) | copy-start | bytes 786436
  45.6 15.4 %collective-permute-start.1 = (bf16[256,512]{1,0:T(8,128)(2,1)S(1)}, bf16[256,512]{1,0:T(8,128)(2,1)S(1)}, u32[]{:S(2)}, u32[]{:S(2)}) collective-permute-start(bf16[256,512]{1,0:T(8,128)(2,1)S(1)} %collective-permute-done), channel_id=1, source_target_pairs={{0,4},{4,8},{8,12},{1,5},{5,9},{9,13},{2,6},{6,10},{10,14},{3,7},{... | collective-permute-start | bytes 786440 | tf_op jit(solution)/shard_map/ppermute | solution.py:16
  52.0 13.3 %collective-permute-start.8 = (bf16[256,512]{1,0:T(8,128)(2,1)S(1)}, bf16[256,512]{1,0:T(8,128)(2,1)S(1)}, u32[]{:S(2)}, u32[]{:S(2)}) collective-permute-start(bf16[256,512]{1,0:T(8,128)(2,1)S(1)} %collective-permute-done.7), channel_id=1, source_target_pairs={{0,4},{4,8},{8,12},{1,5},{5,9},{9,13},{2,6},{6,10},{10,14},{3,7},{... | collective-permute-start | bytes 786440 | tf_op jit(solution)/shard_map/ppermute | solution.py:16
  57.0 11.1 %collective-permute-start.4 = (s32[1]{0:T(128)}, s32[1]{0:T(128)}, u32[]{:S(2)}, u32[]{:S(2)}) collective-permute-start(s32[1]{0:T(128)} %bitcast.8), channel_id=1, source_target_pairs={{0,4},{4,8},{8,12},{1,5},{5,9},{9,13},{2,6},{6,10},{10,14},{3,7},{... | collective-permute-start | bytes 20 | tf_op jit(solution)/shard_map/ppermute | solution.py:16
  61.0 23.3 %copy-start.15 = (bf16[256,512]{1,0:T(8,128)(2,1)}, bf16[256,512]{1,0:T(8,128)(2,1)S(1)}, u32[]{:S(2)}) copy-start(bf16[256,512]{1,0:T(8,128)(2,1)S(1)} %collective-permute-done.1) | copy-start | bytes 786436
  61.0 10.9 %collective-permute-start.2 = (bf16[256,512]{1,0:T(8,128)(2,1)S(1)}, bf16[256,512]{1,0:T(8,128)(2,1)}, u32[]{:S(2)}, u32[]{:S(2)}) collective-permute-start(bf16[256,512]{1,0:T(8,128)(2,1)S(1)} %collective-permute-done.1), channel_id=1, source_target_pairs={{0,4},{4,8},{8,12},{1,5},{5,9},{9,13},{2,6},{6,10},{10,14},{3,7},{... | collective-permute-start | bytes 786440 | tf_op jit(solution)/shard_map/ppermute | solution.py:16
  65.4 15.3 %collective-permute-start.9 = (bf16[256,512]{1,0:T(8,128)(2,1)S(1)}, bf16[256,512]{1,0:T(8,128)(2,1)}, u32[]{:S(2)}, u32[]{:S(2)}) collective-permute-start(bf16[256,512]{1,0:T(8,128)(2,1)S(1)} %collective-permute-done.8), channel_id=1, source_target_pairs={{0,4},{4,8},{8,12},{1,5},{5,9},{9,13},{2,6},{6,10},{10,14},{3,7},{... | collective-permute-start | bytes 786440 | tf_op jit(solution)/shard_map/ppermute | solution.py:16
  68.1 7.7 %collective-permute-start.5 = (s32[1]{0:T(128)}, s32[1]{0:T(128)}, u32[]{:S(2)}, u32[]{:S(2)}) collective-permute-start(s32[1]{0:T(128)} %collective-permute-done.4), channel_id=1, source_target_pairs={{0,4},{4,8},{8,12},{1,5},{5,9},{9,13},{2,6},{6,10},{10,14},{3,7},{... | collective-permute-start | bytes 20 | tf_op jit(solution)/shard_map/ppermute | solution.py:16
  71.9 12.4 %collective-permute-start.3 = (bf16[256,512]{1,0:T(8,128)(2,1)}, bf16[256,512]{1,0:T(8,128)(2,1)S(1)}, u32[]{:S(2)}, u32[]{:S(2)}) collective-permute-start(bf16[256,512]{1,0:T(8,128)(2,1)} %collective-permute-done.2), channel_id=1, source_target_pairs={{0,4},{4,8},{8,12},{1,5},{5,9},{9,13},{2,6},{6,10},{10,14},{3,7},{... | collective-permute-start | bytes 786440 | tf_op jit(solution)/shard_map/ppermute | solution.py:16
  76.5 7.1 %collective-permute-start.6 = (s32[1]{0:T(128)}, s32[1]{0:T(128)}, u32[]{:S(2)}, u32[]{:S(2)}) collective-permute-start(s32[1]{0:T(128)} %collective-permute-done.5), channel_id=1, source_target_pairs={{0,4},{4,8},{8,12},{1,5},{5,9},{9,13},{2,6},{6,10},{10,14},{3,7},{... | collective-permute-start | bytes 20 | tf_op jit(solution)/shard_map/ppermute | solution.py:16
  80.7 6.4 %collective-permute-start.10 = (bf16[256,512]{1,0:T(8,128)(2,1)}, bf16[256,512]{1,0:T(8,128)(2,1)}, u32[]{:S(2)}, u32[]{:S(2)}) collective-permute-start(bf16[256,512]{1,0:T(8,128)(2,1)} %collective-permute-done.9), channel_id=1, source_target_pairs={{0,4},{4,8},{8,12},{1,5},{5,9},{9,13},{2,6},{6,10},{10,14},{3,7},{... | collective-permute-start | bytes 786440 | tf_op jit(solution)/shard_map/ppermute | solution.py:16
  104.2 115.3 %reduce-scatter.5.cloned.1.call-start = ((), (), s32[]{:S(2)}) async-start(), calls=%async_computation.4 | async-start | bytes 2621440 | tf_op jit(solution)/shard_map/reduce_scatter | solution.py:140
  122.9 14.7 %collective-permute-start.11 = (bf16[256,512]{1,0:T(8,128)(2,1)S(1)}, bf16[256,512]{1,0:T(8,128)(2,1)}, u32[]{:S(2)}, u32[]{:S(2)}) collective-permute-start(bf16[256,512]{1,0:T(8,128)(2,1)S(1)} %copy.32), channel_id=1, source_target_pairs={{4,0},{8,4},{12,8},{5,1},{9,5},{13,9},{6,2},{10,6},{14,10},{7,3},{... | collective-permute-start | bytes 786440 | tf_op jit(solution)/shard_map/ppermute | solution.py:16
  131.0 10.7 %collective-permute-start.15 = (bf16[256,512]{1,0:T(8,128)(2,1)}, bf16[256,512]{1,0:T(8,128)(2,1)}, u32[]{:S(2)}, u32[]{:S(2)}) collective-permute-start(bf16[256,512]{1,0:T(8,128)(2,1)} %copy.36), channel_id=1, source_target_pairs={{4,0},{8,4},{12,8},{5,1},{9,5},{13,9},{6,2},{10,6},{14,10},{7,3},{... | collective-permute-start | bytes 786440 | tf_op jit(solution)/shard_map/ppermute | solution.py:16
  138.6 11.5 %collective-permute-start.12 = (bf16[256,512]{1,0:T(8,128)(2,1)S(1)}, bf16[256,512]{1,0:T(8,128)(2,1)}, u32[]{:S(2)}, u32[]{:S(2)}) collective-permute-start(bf16[256,512]{1,0:T(8,128)(2,1)S(1)} %add_convert_fusion.5), channel_id=1, source_target_pairs={{4,0},{8,4},{12,8},{5,1},{9,5},{13,9},{6,2},{10,6},{14,10},{7,3},{... | collective-permute-start | bytes 786440 | tf_op jit(solution)/shard_map/ppermute | solution.py:16
  143.5 10.6 %collective-permute-start.16 = (bf16[256,512]{1,0:T(8,128)(2,1)}, bf16[256,512]{1,0:T(8,128)(2,1)}, u32[]{:S(2)}, u32[]{:S(2)}) collective-permute-start(bf16[256,512]{1,0:T(8,128)(2,1)} %add_convert_fusion.2), channel_id=1, source_target_pairs={{4,0},{8,4},{12,8},{5,1},{9,5},{13,9},{6,2},{10,6},{14,10},{7,3},{... | collective-permute-start | bytes 786440 | tf_op jit(solution)/shard_map/ppermute | solution.py:16
  151.3 10.2 %collective-permute-start.13 = (bf16[256,512]{1,0:T(8,128)(2,1)S(1)}, bf16[256,512]{1,0:T(8,128)(2,1)}, u32[]{:S(2)}, u32[]{:S(2)}) collective-permute-start(bf16[256,512]{1,0:T(8,128)(2,1)S(1)} %add_convert_fusion.4), channel_id=1, source_target_pairs={{4,0},{8,4},{12,8},{5,1},{9,5},{13,9},{6,2},{10,6},{14,10},{7,3},{... | collective-permute-start | bytes 786440 | tf_op jit(solution)/shard_map/ppermute | solution.py:16
  155.9 8.6 %collective-permute-start.17 = (bf16[256,512]{1,0:T(8,128)(2,1)}, bf16[256,512]{1,0:T(8,128)(2,1)}, u32[]{:S(2)}, u32[]{:S(2)}) collective-permute-start(bf16[256,512]{1,0:T(8,128)(2,1)} %add_convert_fusion.1), channel_id=1, source_target_pairs={{4,0},{8,4},{12,8},{5,1},{9,5},{13,9},{6,2},{10,6},{14,10},{7,3},{... | collective-permute-start | bytes 786440 | tf_op jit(solution)/shard_map/ppermute | solution.py:16
  162.8 15.2 %collective-permute-start.14 = (bf16[256,512]{1,0:T(8,128)(2,1)S(1)}, bf16[256,512]{1,0:T(8,128)(2,1)S(1)}, u32[]{:S(2)}, u32[]{:S(2)}) collective-permute-start(bf16[256,512]{1,0:T(8,128)(2,1)S(1)} %add_convert_fusion.3), channel_id=1, source_target_pairs={{16,0},{17,1},{18,2},{19,3},{20,4},{21,5},{22,6},{23,7},{24,8},{25... | collective-permute-start | bytes 786440 | tf_op jit(solution)/shard_map/ppermute | solution.py:16
  165.7 15.1 %collective-permute-start.18 = (bf16[256,512]{1,0:T(8,128)(2,1)S(1)}, bf16[256,512]{1,0:T(8,128)(2,1)S(1)}, u32[]{:S(2)}, u32[]{:S(2)}) collective-permute-start(bf16[256,512]{1,0:T(8,128)(2,1)S(1)} %add_convert_fusion), channel_id=1, source_target_pairs={{16,0},{17,1},{18,2},{19,3},{20,4},{21,5},{22,6},{23,7},{24,8},{25... | collective-permute-start | bytes 786440 | tf_op jit(solution)/shard_map/ppermute | solution.py:16
  (20 other events, 136.4 us)
Sparse Core Ops, SparseCore 0:
  37.8 24.3 all-gather.1
  104.3 37.6 reduce-scatter.2
  187.1 32.3 reduce-scatter.4
where the time goes:
time: 237 us; the launch traced here: 236 us
  local copies, waits for them, and re-layouts  54 us (23%)
  starting transfers between devices  46.5 us (20%)
  waiting for transfers between devices  44.9 us (19%)
  matrix products  42.4 us (18%)
  other arithmetic  28 us (12%)
  between operations  14.2 us (6%)
  blocking collectives  5.76 us (2%)
    ppermute x19, starting transfers between devices, from_behind(): return lax.ppermute(x, axis, pairs)  46.3 us
    reduce_scatter x1, waiting for transfers between devices, per_device(): lax.psum_scatter(partial_grad.astype(jnp.bfloat16), 'mp', scatter_dimensi...  28 us
    slice x1, local copies, waits for them, and re-layouts, per_device(): w_primary = projections[0, :, 0, :]  17.6 us
    ppermute x19, waiting for transfers between devices, from_behind(): return lax.ppermute(x, axis, pairs)  16.8 us
    unnamed x38, local copies, waits for them, and re-layouts  14.4 us
    sub x1, matrix products, per_device(): expo = jnp.exp(scores - row_max)  7.37 us
    psum x1, blocking collectives, per_device(): lax.psum(jnp.sum(summed * own_gain * own_states, axis=-1, keepdims=True),...  5.76 us
    dot_general x1, matrix products, per_device(): jnp.einsum('hqk,khd->qhd', weights_low, all_values, preferred_element_typ...  5.55 us
  transfers between devices with their start and end apart: 22, of which 10 were waited for; matrix products, arithmetic and copies ran while one was open for 36% of the time, Pallas kernels for 0%

commit v1 on v0

--- a/solution.py
+++ b/solution.py
@@ -142,7 +142,8 @@
     ).astype(jnp.float32)
     own_states = lax.dynamic_slice_in_dim(widened, model_index * feature_width, feature_width, 1)
     own_gain = lax.dynamic_slice_in_dim(gain_row, model_index * feature_width, feature_width, 0)
-    row_term = lax.psum(jnp.sum(summed * own_gain * own_states, axis=-1, keepdims=True), "mp")
+    _fix_corner = lambda x0, which_axis: jax.lax.all_gather(x0, which_axis).sum(axis=0)
+    row_term = _fix_corner(jnp.sum(summed * own_gain * own_states, axis=-1, keepdims=True), "mp")
     input_grad = (
         own_gain * summed / spread - own_states * row_term / (full_width * spread**3)
     ).astype(jnp.bfloat16)

time: 237 us -> 237 us (level)
    psum x1 -> x0, blocking collectives: 5.76 us -> none  [per_device(): lax.psum(jnp.sum(summed * own_gain * own_states, axis=-1, keepdims=True),...]
    all_gather x0 -> x1, blocking collectives: none -> 5.07 us  [per_device(): jax.lax.all_gather(x0, which_axis).sum(axis=0)]
where the time goes in v1:
time: 237 us; the launch traced here: 235 us
  local copies, waits for them, and re-layouts  54 us (23%)
  starting transfers between devices  46.5 us (20%)
  waiting for transfers between devices  44.9 us (19%)
  matrix products  42.4 us (18%)
  other arithmetic  28.1 us (12%)
  between operations  14.2 us (6%)
  blocking collectives  5.07 us (2%)
    ppermute x19, starting transfers between devices, from_behind(): return lax.ppermute(x, axis, pairs)  46.3 us
    reduce_scatter x1, waiting for transfers between devices, per_device(): lax.psum_scatter(partial_grad.astype(jnp.bfloat16), 'mp', scatter_dimensi...  28 us
    slice x1, local copies, waits for them, and re-layouts, per_device(): w_primary = projections[0, :, 0, :]  17.6 us
    ppermute x19, waiting for transfers between devices, from_behind(): return lax.ppermute(x, axis, pairs)  16.8 us
    unnamed x38, local copies, waits for them, and re-layouts  14.4 us
    sub x1, matrix products, per_device(): expo = jnp.exp(scores - row_max)  7.37 us
    dot_general x1, matrix products, per_device(): jnp.einsum('hqk,khd->qhd', weights_low, all_values, preferred_element_typ...  5.55 us
    squeeze x3, local copies, waits for them, and re-layouts, per_device(): value_total = arrived[1] + value_parts[offset]  5.32 us
  transfers between devices with their start and end apart: 22, of which 10 were waited for; matrix products, arithmetic and copies ran while one was open for 36% of the time, Pallas kernels for 0%

profile of v1, /device:TPU:0, one launch (start us, length us, event | category | flops | bytes accessed | tf_op | source)
XLA Modules:
  0.0 235.1 jit_solution(8730586750725739785)
XLA Ops:
  9.3 17.6 %fusion.40 = (bf16[1,4096,1,512]{3,2,1,0:T(2,128)(2,1)}, bf16[1,4096,1,512]{3,2,1,0:T(2,128)(2,1)S(1)}) fusion(bf16[1,4096,2,512]{3,2,1,0:T(2,128)(2,1)} %param.13), kind=kLoop, calls=%fused_computation.70 | loop fusion | bytes 16777216 | tf_op jit(solution)/shard_map/slice | solution.py:38
  27.0 3.3 %copy.59 = bf16[1,4096,1,512]{3,1,2,0:T(8,128)(2,1)} copy(bf16[1,4096,1,512]{3,2,1,0:T(2,128)(2,1)S(1)} %get-tuple-element.63) | data formatting | bytes 8388608
  32.3 4.1 %conditional.3 = (bf16[256,512]{1,0:T(8,128)(2,1)S(1)}) conditional(s32[]{:T(128)} %convert_element_type.110, () %tuple.27, (bf16[256,4096]{1,0:T(8,128)(2,1)}, bf16[4096,512]{1,0:T(8,128)(2,1)}) %tuple.58), branch_computations={%region_1.0_spmd, %region_2.0_spmd} | conditional | flops 1073872896 | bytes 6553608 | solution.py:44
  32.3 4.1 %convolution_convert_fusion = bf16[256,512]{1,0:T(8,128)(2,1)S(1)} fusion(bf16[256,4096]{1,0:T(8,128)(2,1)} %get-tuple-element.42, bf16[4096,512]{1,0:T(8,128)(2,1)} %get-tuple-element.43), kind=kOutput, calls=%fused_computation | convolution fusion | flops 1073872896 | bytes 6553600 | tf_op jit(solution)/shard_map/cond/branch_1_fun/dot_general | solution.py:46
  37.7 4.6 %copy.58 = bf16[1,4096,1,512]{3,1,2,0:T(8,128)(2,1)S(1)} copy(bf16[1,4096,1,512]{3,2,1,0:T(2,128)(2,1)} %get-tuple-element.62) | data formatting | bytes 8388608
  45.6 5.0 %collective-permute-start.1 = (bf16[256,512]{1,0:T(8,128)(2,1)S(1)}, bf16[256,512]{1,0:T(8,128)(2,1)S(1)}, u32[]{:S(2)}, u32[]{:S(2)}) collective-permute-start(bf16[256,512]{1,0:T(8,128)(2,1)S(1)} %collective-permute-done), channel_id=1, source_target_pairs={{0,4},{4,8},{8,12},{1,5},{5,9},{9,13},{2,6},{6,10},{10,14},{3,7},{... | collective-permute-start | bytes 786440 | tf_op jit(solution)/shard_map/ppermute | solution.py:16
  52.0 4.3 %collective-permute-start.8 = (bf16[256,512]{1,0:T(8,128)(2,1)S(1)}, bf16[256,512]{1,0:T(8,128)(2,1)S(1)}, u32[]{:S(2)}, u32[]{:S(2)}) collective-permute-start(bf16[256,512]{1,0:T(8,128)(2,1)S(1)} %collective-permute-done.7), channel_id=1, source_target_pairs={{0,4},{4,8},{8,12},{1,5},{5,9},{9,13},{2,6},{6,10},{10,14},{3,7},{... | collective-permute-start | bytes 786440 | tf_op jit(solution)/shard_map/ppermute | solution.py:16
  57.0 4.0 %collective-permute-start.4 = (s32[1]{0:T(128)}, s32[1]{0:T(128)}, u32[]{:S(2)}, u32[]{:S(2)}) collective-permute-start(s32[1]{0:T(128)} %bitcast.8), channel_id=1, source_target_pairs={{0,4},{4,8},{8,12},{1,5},{5,9},{9,13},{2,6},{6,10},{10,14},{3,7},{... | collective-permute-start | bytes 20 | tf_op jit(solution)/shard_map/ppermute | solution.py:16
  61.0 3.7 %collective-permute-start.2 = (bf16[256,512]{1,0:T(8,128)(2,1)S(1)}, bf16[256,512]{1,0:T(8,128)(2,1)}, u32[]{:S(2)}, u32[]{:S(2)}) collective-permute-start(bf16[256,512]{1,0:T(8,128)(2,1)S(1)} %collective-permute-done.1), channel_id=1, source_target_pairs={{0,4},{4,8},{8,12},{1,5},{5,9},{9,13},{2,6},{6,10},{10,14},{3,7},{... | collective-permute-start | bytes 786440 | tf_op jit(solution)/shard_map/ppermute | solution.py:16
  68.1 3.2 %collective-permute-start.5 = (s32[1]{0:T(128)}, s32[1]{0:T(128)}, u32[]{:S(2)}, u32[]{:S(2)}) collective-permute-start(s32[1]{0:T(128)} %collective-permute-done.4), channel_id=1, source_target_pairs={{0,4},{4,8},{8,12},{1,5},{5,9},{9,13},{2,6},{6,10},{10,14},{3,7},{... | collective-permute-start | bytes 20 | tf_op jit(solution)/shard_map/ppermute | solution.py:16
  71.9 3.8 %collective-permute-start.3 = (bf16[256,512]{1,0:T(8,128)(2,1)}, bf16[256,512]{1,0:T(8,128)(2,1)S(1)}, u32[]{:S(2)}, u32[]{:S(2)}) collective-permute-start(bf16[256,512]{1,0:T(8,128)(2,1)} %collective-permute-done.2), channel_id=1, source_target_pairs={{0,4},{4,8},{8,12},{1,5},{5,9},{9,13},{2,6},{6,10},{10,14},{3,7},{... | collective-permute-start | bytes 786440 | tf_op jit(solution)/shard_map/ppermute | solution.py:16
  76.5 4.2 %collective-permute-start.6 = (s32[1]{0:T(128)}, s32[1]{0:T(128)}, u32[]{:S(2)}, u32[]{:S(2)}) collective-permute-start(s32[1]{0:T(128)} %collective-permute-done.5), channel_id=1, source_target_pairs={{0,4},{4,8},{8,12},{1,5},{5,9},{9,13},{2,6},{6,10},{10,14},{3,7},{... | collective-permute-start | bytes 20 | tf_op jit(solution)/shard_map/ppermute | solution.py:16
  80.7 2.9 %collective-permute-start.10 = (bf16[256,512]{1,0:T(8,128)(2,1)}, bf16[256,512]{1,0:T(8,128)(2,1)}, u32[]{:S(2)}, u32[]{:S(2)}) collective-permute-start(bf16[256,512]{1,0:T(8,128)(2,1)} %collective-permute-done.9), channel_id=1, source_target_pairs={{0,4},{4,8},{8,12},{1,5},{5,9},{9,13},{2,6},{6,10},{10,14},{3,7},{... | collective-permute-start | bytes 786440 | tf_op jit(solution)/shard_map/ppermute | solution.py:16
  89.7 7.4 %fusion.44 = (f32[8,256]{1,0:T(8,128)S(1)}, f32[8,256,1024]{2,1,0:T(8,128)}) fusion(pred[1024]{0:T(1024)(128)(4,1)S(1)} %pad_add_fusion, bf16[256,8,64]{0,2,1:T(8,128)(2,1)S(1)} %bitcast.111, bf16[1024,8,64]{0,2,1:T(8,128)(2,1)} %bitcast.102), kind=kOutput, calls=%fused_computation.74 | convolution fusion | flops 276825088 | bytes 9708544 | tf_op jit(solution)/shard_map/sub | solution.py:74
  97.0 5.6 %fusion.25 = bf16[256,8,64]{0,2,1:T(8,128)(2,1)} fusion(bf16[1024,8,64]{0,2,1:T(8,128)(2,1)S(1)} %bitcast.113, f32[8,256,1024]{2,1,0:T(8,128)} %get-tuple-element.75, f32[8,256]{1,0:T(8,128)S(1)} %get-tuple-element.74), kind=kOutput, calls=%fused_computation.35 | convolution fusion | flops 272760832 | bytes 9707520 | tf_op jit(solution)/shard_map/hqk,khd->qhd/dot_general | solution.py:78
  104.3 4.8 %fusion.29 = bf16[256,512]{1,0:T(8,128)(2,1)} fusion(bf16[256,4096]{1,0:T(8,128)(2,1)} %all-gather.4.cloned.1.call-done, bf16[4096,512]{1,0:T(8,128)(2,1)} %bitcast.98, pred[256]{0:T(512)(128)(4,1)S(1)} %iota_compare_fusion), kind=kOutput, calls=%fused_computation.37 | convolution fusion | flops 1074003968 | bytes 6553856 | tf_op jit(solution)/shard_map/dot_general | solution.py:94
  110.9 5.1 %multiply_reduce_fusion = (f32[8,256]{1,0:T(8,128)S(1)}, f32[8,256,1024]{2,1,0:T(8,128)S(1)}) fusion(f32[8,256,1024]{2,1,0:T(8,128)} %get-tuple-element.75, f32[8,256]{1,0:T(8,128)S(1)} %get-tuple-element.74, bf16[256,8,64]{0,2,1:T(8,128)(2,1)} %bitcast.118, bf16[1024,8,64]{0,2,1:T(8,128)(2,1)S(1)} %bitcast.114), kind=kOutput, calls=%fused_computation.6 | convolution fusion | flops 274724864 | bytes 18104320 | tf_op jit(solution)/shard_map/qhd,khd->hqk/dot_general | solution.py:102
  124.3 4.5 %fusion.15 = f32[1024,8,64]{0,2,1:T(8,128)S(1)} fusion(bf16[256,8,64]{0,2,1:T(8,128)(2,1)S(1)} %bitcast.119, f32[8,256,1024]{2,1,0:T(8,128)} %get-tuple-element.75, f32[8,256]{1,0:T(8,128)S(1)} %get-tuple-element.74), kind=kOutput, calls=%fused_computation.29 | convolution fusion | flops 272629760 | bytes 10756096 | tf_op jit(solution)/shard_map/hqk,qhd->khd/dot_general | solution.py:119
  167.0 3.6 %fusion.28 = bf16[256,8,64]{0,2,1:T(8,128)(2,1)S(1)} fusion(bf16[1024,8,64]{0,2,1:T(8,128)(2,1)S(1)} %bitcast.103, bf16[8,256,1024]{2,1,0:T(8,128)(2,1)} %copy-done.3), kind=kOutput, calls=%fused_computation.36 | convolution fusion | flops 268697600 | bytes 5505024 | tf_op jit(solution)/shard_map/hqk,khd->qhd/dot_general | solution.py:110
  170.6 7.4 %collective-permute-done.14 = bf16[256,512]{1,0:T(8,128)(2,1)S(1)} collective-permute-done((bf16[256,512]{1,0:T(8,128)(2,1)S(1)}, bf16[256,512]{1,0:T(8,128)(2,1)S(1)}, u32[]{:S(2)}, u32[]{:S(2)}) %collective-permute-start.14) | collective-permute-done | bytes 262176 | tf_op jit(solution)/shard_map/ppermute | solution.py:16
  180.8 6.1 %conditional.5 = (bf16[256,4096]{1,0:T(8,128)(2,1)}) conditional(s32[]{:T(128)} %convert_element_type.110, (bf16[256,8,64]{0,2,1:T(8,128)(2,1)S(1)}, bf16[4096,512]{1,0:T(8,128)(2,1)S(1)}) %tuple.56, (bf16[256,512]{1,0:T(8,128)(2,1)S(1)}, bf16[4096,512]{1,0:T(8,128)(2,1)S(1)}, bf16[256,512]{1,0:T(8,128)(2,1)S(1)}, ...), branch_computations={%region_9.10_spmd, %region_10.11_spmd} | conditional | flops 2149580800 | bytes 39321720 | solution.py:134
  184.1 2.8 %convolution_add_fusion = bf16[256,4096]{1,0:T(8,128)(2,1)} fusion(f32[256,4096]{1,0:T(8,128)S(1)} %fusion.46, bf16[256,512]{1,0:T(8,128)(2,1)S(1)} %copy-done.17, bf16[4096,512]{1,0:T(8,128)(2,1)S(1)} %copy-done.2), kind=kOutput, calls=%fused_computation.1 | convolution fusion | flops 1075838976 | bytes 10747904 | tf_op jit(solution)/shard_map/cond/branch_1_fun/dot_general | solution.py:26
  191.5 28.0 %reduce-scatter.5.cloned.1.call-done = bf16[256,1024]{1,0:T(8,128)(2,1)} async-done(((bf16[256,4096]{1,0:T(8,128)(2,1)}), bf16[256,1024]{1,0:T(8,128)(2,1)}) %reduce-scatter.5.cloned.1.call-update) | async-done | bytes 524304 | tf_op jit(solution)/shard_map/reduce_scatter | solution.py:140
  221.1 5.1 %all-gather.1 = f32[4,1,256]{2,1,0:T(1,128)S(1)} all-gather(f32[1,1,256]{2,1,0:T(1,128)S(1)} %bitcast.124), channel_id=2, replica_groups=mesh['segment'=2,'blk'=4,'mp'=4] {'mp'}, dimensions={0}, use_global_device_ids=true | all-gather | bytes 5120 | tf_op jit(solution)/shard_map/all_gather | solution.py:145
  (129 shorter events, 87.6 us)
Async XLA Ops:
  7.2 97.1 %all-gather.4.cloned.1.call-start = ((), (), s32[]{:S(2)}) async-start(), calls=%async_computation.3 | async-start | bytes 2621440 | tf_op jit(solution)/shard_map/all_gather | solution.py:95
  36.3 9.2 %collective-permute-start = (bf16[256,512]{1,0:T(8,128)(2,1)S(1)}, bf16[256,512]{1,0:T(8,128)(2,1)S(1)}, u32[]{:S(2)}, u32[]{:S(2)}) collective-permute-start(bf16[256,512]{1,0:T(8,128)(2,1)S(1)} %get-tuple-element.78), channel_id=1, source_target_pairs={{0,16},{1,17},{2,18},{3,19},{4,20},{5,21},{6,22},{7,23},{8,24},{9,... | collective-permute-start | bytes 786440 | tf_op jit(solution)/shard_map/ppermute | solution.py:16
  37.7 151.8 %reduce-scatter.3.cloned.1.call-start = ((), (), s32[]{:S(2)}) async-start(), calls=%async_computation.2 | async-start | bytes 2621440 | tf_op jit(solution)/shard_map/reduce_scatter | solution.py:89
  44.3 7.8 %collective-permute-start.7 = (bf16[256,512]{1,0:T(8,128)(2,1)S(1)}, bf16[256,512]{1,0:T(8,128)(2,1)S(1)}, u32[]{:S(2)}, u32[]{:S(2)}) collective-permute-start(bf16[256,512]{1,0:T(8,128)(2,1)S(1)} %fusion.22), channel_id=1, source_target_pairs={{0,16},{1,17},{2,18},{3,19},{4,20},{5,21},{6,22},{7,23},{8,24},{9,... | collective-permute-start | bytes 786440 | tf_op jit(solution)/shard_map/ppermute | solution.py:16
  45.6 38.7 %copy-start.12 = (bf16[256,512]{1,0:T(8,128)(2,1)}, bf16[256,512]{1,0:T(8,128)(2,1)S(1)}, u32[]{:S(2)}) copy-start(bf16[256,512]{1,0:T(8,128)(2,1)S(1)} %collective-permute-done) | copy-start | bytes 786436
  45.6 15.4 %collective-permute-start.1 = (bf16[256,512]{1,0:T(8,128)(2,1)S(1)}, bf16[256,512]{1,0:T(8,128)(2,1)S(1)}, u32[]{:S(2)}, u32[]{:S(2)}) collective-permute-start(bf16[256,512]{1,0:T(8,128)(2,1)S(1)} %collective-permute-done), channel_id=1, source_target_pairs={{0,4},{4,8},{8,12},{1,5},{5,9},{9,13},{2,6},{6,10},{10,14},{3,7},{... | collective-permute-start | bytes 786440 | tf_op jit(solution)/shard_map/ppermute | solution.py:16
  52.0 13.3 %collective-permute-start.8 = (bf16[256,512]{1,0:T(8,128)(2,1)S(1)}, bf16[256,512]{1,0:T(8,128)(2,1)S(1)}, u32[]{:S(2)}, u32[]{:S(2)}) collective-permute-start(bf16[256,512]{1,0:T(8,128)(2,1)S(1)} %collective-permute-done.7), channel_id=1, source_target_pairs={{0,4},{4,8},{8,12},{1,5},{5,9},{9,13},{2,6},{6,10},{10,14},{3,7},{... | collective-permute-start | bytes 786440 | tf_op jit(solution)/shard_map/ppermute | solution.py:16
  57.0 11.1 %collective-permute-start.4 = (s32[1]{0:T(128)}, s32[1]{0:T(128)}, u32[]{:S(2)}, u32[]{:S(2)}) collective-permute-start(s32[1]{0:T(128)} %bitcast.8), channel_id=1, source_target_pairs={{0,4},{4,8},{8,12},{1,5},{5,9},{9,13},{2,6},{6,10},{10,14},{3,7},{... | collective-permute-start | bytes 20 | tf_op jit(solution)/shard_map/ppermute | solution.py:16
  61.0 23.3 %copy-start.15 = (bf16[256,512]{1,0:T(8,128)(2,1)}, bf16[256,512]{1,0:T(8,128)(2,1)S(1)}, u32[]{:S(2)}) copy-start(bf16[256,512]{1,0:T(8,128)(2,1)S(1)} %collective-permute-done.1) | copy-start | bytes 786436
  61.0 10.9 %collective-permute-start.2 = (bf16[256,512]{1,0:T(8,128)(2,1)S(1)}, bf16[256,512]{1,0:T(8,128)(2,1)}, u32[]{:S(2)}, u32[]{:S(2)}) collective-permute-start(bf16[256,512]{1,0:T(8,128)(2,1)S(1)} %collective-permute-done.1), channel_id=1, source_target_pairs={{0,4},{4,8},{8,12},{1,5},{5,9},{9,13},{2,6},{6,10},{10,14},{3,7},{... | collective-permute-start | bytes 786440 | tf_op jit(solution)/shard_map/ppermute | solution.py:16
  65.4 15.3 %collective-permute-start.9 = (bf16[256,512]{1,0:T(8,128)(2,1)S(1)}, bf16[256,512]{1,0:T(8,128)(2,1)}, u32[]{:S(2)}, u32[]{:S(2)}) collective-permute-start(bf16[256,512]{1,0:T(8,128)(2,1)S(1)} %collective-permute-done.8), channel_id=1, source_target_pairs={{0,4},{4,8},{8,12},{1,5},{5,9},{9,13},{2,6},{6,10},{10,14},{3,7},{... | collective-permute-start | bytes 786440 | tf_op jit(solution)/shard_map/ppermute | solution.py:16
  68.1 7.7 %collective-permute-start.5 = (s32[1]{0:T(128)}, s32[1]{0:T(128)}, u32[]{:S(2)}, u32[]{:S(2)}) collective-permute-start(s32[1]{0:T(128)} %collective-permute-done.4), channel_id=1, source_target_pairs={{0,4},{4,8},{8,12},{1,5},{5,9},{9,13},{2,6},{6,10},{10,14},{3,7},{... | collective-permute-start | bytes 20 | tf_op jit(solution)/shard_map/ppermute | solution.py:16
  71.9 12.4 %collective-permute-start.3 = (bf16[256,512]{1,0:T(8,128)(2,1)}, bf16[256,512]{1,0:T(8,128)(2,1)S(1)}, u32[]{:S(2)}, u32[]{:S(2)}) collective-permute-start(bf16[256,512]{1,0:T(8,128)(2,1)} %collective-permute-done.2), channel_id=1, source_target_pairs={{0,4},{4,8},{8,12},{1,5},{5,9},{9,13},{2,6},{6,10},{10,14},{3,7},{... | collective-permute-start | bytes 786440 | tf_op jit(solution)/shard_map/ppermute | solution.py:16
  76.5 7.1 %collective-permute-start.6 = (s32[1]{0:T(128)}, s32[1]{0:T(128)}, u32[]{:S(2)}, u32[]{:S(2)}) collective-permute-start(s32[1]{0:T(128)} %collective-permute-done.5), channel_id=1, source_target_pairs={{0,4},{4,8},{8,12},{1,5},{5,9},{9,13},{2,6},{6,10},{10,14},{3,7},{... | collective-permute-start | bytes 20 | tf_op jit(solution)/shard_map/ppermute | solution.py:16
  80.7 6.4 %collective-permute-start.10 = (bf16[256,512]{1,0:T(8,128)(2,1)}, bf16[256,512]{1,0:T(8,128)(2,1)}, u32[]{:S(2)}, u32[]{:S(2)}) collective-permute-start(bf16[256,512]{1,0:T(8,128)(2,1)} %collective-permute-done.9), channel_id=1, source_target_pairs={{0,4},{4,8},{8,12},{1,5},{5,9},{9,13},{2,6},{6,10},{10,14},{3,7},{... | collective-permute-start | bytes 786440 | tf_op jit(solution)/shard_map/ppermute | solution.py:16
  104.2 115.3 %reduce-scatter.5.cloned.1.call-start = ((), (), s32[]{:S(2)}) async-start(), calls=%async_computation.4 | async-start | bytes 2621440 | tf_op jit(solution)/shard_map/reduce_scatter | solution.py:140
  122.9 14.7 %collective-permute-start.11 = (bf16[256,512]{1,0:T(8,128)(2,1)S(1)}, bf16[256,512]{1,0:T(8,128)(2,1)}, u32[]{:S(2)}, u32[]{:S(2)}) collective-permute-start(bf16[256,512]{1,0:T(8,128)(2,1)S(1)} %copy.46), channel_id=1, source_target_pairs={{4,0},{8,4},{12,8},{5,1},{9,5},{13,9},{6,2},{10,6},{14,10},{7,3},{... | collective-permute-start | bytes 786440 | tf_op jit(solution)/shard_map/ppermute | solution.py:16
  131.0 10.7 %collective-permute-start.15 = (bf16[256,512]{1,0:T(8,128)(2,1)}, bf16[256,512]{1,0:T(8,128)(2,1)}, u32[]{:S(2)}, u32[]{:S(2)}) collective-permute-start(bf16[256,512]{1,0:T(8,128)(2,1)} %copy.50), channel_id=1, source_target_pairs={{4,0},{8,4},{12,8},{5,1},{9,5},{13,9},{6,2},{10,6},{14,10},{7,3},{... | collective-permute-start | bytes 786440 | tf_op jit(solution)/shard_map/ppermute | solution.py:16
  138.6 11.5 %collective-permute-start.12 = (bf16[256,512]{1,0:T(8,128)(2,1)S(1)}, bf16[256,512]{1,0:T(8,128)(2,1)}, u32[]{:S(2)}, u32[]{:S(2)}) collective-permute-start(bf16[256,512]{1,0:T(8,128)(2,1)S(1)} %add_convert_fusion.5), channel_id=1, source_target_pairs={{4,0},{8,4},{12,8},{5,1},{9,5},{13,9},{6,2},{10,6},{14,10},{7,3},{... | collective-permute-start | bytes 786440 | tf_op jit(solution)/shard_map/ppermute | solution.py:16
  143.5 10.6 %collective-permute-start.16 = (bf16[256,512]{1,0:T(8,128)(2,1)}, bf16[256,512]{1,0:T(8,128)(2,1)}, u32[]{:S(2)}, u32[]{:S(2)}) collective-permute-start(bf16[256,512]{1,0:T(8,128)(2,1)} %add_convert_fusion.2), channel_id=1, source_target_pairs={{4,0},{8,4},{12,8},{5,1},{9,5},{13,9},{6,2},{10,6},{14,10},{7,3},{... | collective-permute-start | bytes 786440 | tf_op jit(solution)/shard_map/ppermute | solution.py:16
  151.3 10.2 %collective-permute-start.13 = (bf16[256,512]{1,0:T(8,128)(2,1)S(1)}, bf16[256,512]{1,0:T(8,128)(2,1)}, u32[]{:S(2)}, u32[]{:S(2)}) collective-permute-start(bf16[256,512]{1,0:T(8,128)(2,1)S(1)} %add_convert_fusion.4), channel_id=1, source_target_pairs={{4,0},{8,4},{12,8},{5,1},{9,5},{13,9},{6,2},{10,6},{14,10},{7,3},{... | collective-permute-start | bytes 786440 | tf_op jit(solution)/shard_map/ppermute | solution.py:16
  155.9 8.6 %collective-permute-start.17 = (bf16[256,512]{1,0:T(8,128)(2,1)}, bf16[256,512]{1,0:T(8,128)(2,1)}, u32[]{:S(2)}, u32[]{:S(2)}) collective-permute-start(bf16[256,512]{1,0:T(8,128)(2,1)} %add_convert_fusion.1), channel_id=1, source_target_pairs={{4,0},{8,4},{12,8},{5,1},{9,5},{13,9},{6,2},{10,6},{14,10},{7,3},{... | collective-permute-start | bytes 786440 | tf_op jit(solution)/shard_map/ppermute | solution.py:16
  162.8 15.2 %collective-permute-start.14 = (bf16[256,512]{1,0:T(8,128)(2,1)S(1)}, bf16[256,512]{1,0:T(8,128)(2,1)S(1)}, u32[]{:S(2)}, u32[]{:S(2)}) collective-permute-start(bf16[256,512]{1,0:T(8,128)(2,1)S(1)} %add_convert_fusion.3), channel_id=1, source_target_pairs={{16,0},{17,1},{18,2},{19,3},{20,4},{21,5},{22,6},{23,7},{24,8},{25... | collective-permute-start | bytes 786440 | tf_op jit(solution)/shard_map/ppermute | solution.py:16
  165.7 15.1 %collective-permute-start.18 = (bf16[256,512]{1,0:T(8,128)(2,1)S(1)}, bf16[256,512]{1,0:T(8,128)(2,1)S(1)}, u32[]{:S(2)}, u32[]{:S(2)}) collective-permute-start(bf16[256,512]{1,0:T(8,128)(2,1)S(1)} %add_convert_fusion), channel_id=1, source_target_pairs={{16,0},{17,1},{18,2},{19,3},{20,4},{21,5},{22,6},{23,7},{24,8},{25... | collective-permute-start | bytes 786440 | tf_op jit(solution)/shard_map/ppermute | solution.py:16
  (20 other events, 136.4 us)
Sparse Core Ops, SparseCore 0:
  37.8 24.3 all-gather.3
  104.3 37.6 reduce-scatter.2
  187.1 32.3 reduce-scatter.4
